TPU v7x, 512 devices: a whole 4x4x16 slice. The times are simulated.
512 devices in a mesh: row: 16 (over y, x), col: 32 (over z, core).
Axes of the slice: x: 4, y: 4, z: 16, core: 2. Of those that a mesh axis runs over, the one named last changes fastest.
Arguments:
- tokens: bfloat16 [4096, 8192], P('row', 'col'), may hold values from -6 to 6
- w_in: bfloat16 [8192, 3, 8192], P('row', None, 'col'), may hold values from -0.0625 to 0.0625
- filt_in: float32 [7, 3, 8192], P(None, None, 'col'), may hold values from -2.4 to 2.4
- filt_mix: float32 [7, 8192], P(None, 'col'), may hold values from -2.4 to 2.4
Outputs:
- gated: bfloat16 [4096, 8192], P('row', 'col')
All inputs are finite; a program needn't handle non-finite values.
Results may differ from a plain program's by a relative error of at most 0.0064.
Values may be sent and summed in bfloat16 or wider, within the bound.
A program may use at most 64 MiB of HBM per device.

v0:
```python
import jax
import jax.numpy as jnp
from jax import lax
from jax.sharding import PartitionSpec as P


def passed_along(block, axis, distance):
    devices = range(lax.axis_size(axis))
    route = [(i - distance, i) for i in devices if i - distance in devices]
    return lax.ppermute(block, axis, route)


def taps(ext, filt, count):
    total = filt[0] * ext[6 : 6 + count]
    for shift_s in range(1, 7):
        total = total + filt[shift_s] * ext[6 - shift_s : 6 - shift_s + count]
    return total


def per_device(tokens, w_in, filt_in, filt_mix):
    rows = tokens.shape[0]
    cols = w_in.shape[2]
    strip = lax.all_gather(tokens, "col", axis=1, tiled=True)
    piece = lax.all_gather(w_in, "row", axis=0, tiled=True)
    flat_piece = piece.reshape(piece.shape[0], 3 * cols)
    summed = jnp.dot(strip, flat_piece, preferred_element_type=jnp.float32)
    proj = summed.astype(jnp.bfloat16).reshape(rows, 3, cols)
    starts_seq = lax.axis_index("row") == 0
    keep_f = jnp.where(starts_seq, 0.0, 1.0).astype(jnp.float32)
    rim = passed_along(proj[rows - 6 :], "row", 1)
    ext = jnp.concatenate([rim.astype(jnp.float32) * keep_f, proj.astype(jnp.float32)], axis=0)
    conv = taps(ext, filt_in, rows)
    prod = conv[:, 1] * conv[:, 2]
    prod_rim = passed_along(prod[rows - 6 :], "row", 1)
    ext_prod = jnp.concatenate([prod_rim * keep_f, prod], axis=0)
    mix = taps(ext_prod, filt_mix, rows)
    query = conv[:, 0]
    return (query * mix).astype(jnp.bfloat16)


def solution(mesh):
    return jax.shard_map(
        per_device,
        mesh=mesh,
        in_specs=(P("row", "col"), P("row", None, "col"), P(None, None, "col"), P(None, "col")),
        out_specs=P("row", "col"),
        check_vma=False,
    )
```

profile of v0, /device:TPU:8, one launch (start us, length us, event | category | flops | bytes accessed | tf_op | source)
XLA Modules:
  0.0 247.7 jit_solution(13775816980189097958)
XLA Ops:
  6.5 0.0 all-gather.3.cloned.1.call-start
  6.5 0.7 all-gather.3.cloned.1.call-update
  7.3 0.0 all-gather.5.cloned.1.call-start
  7.3 2.3 copy.8
  9.6 0.0 all-gather.5.cloned.1.call-update
  9.6 1.0 fusion.36
  10.7 83.2 %all-gather.3.cloned.1.call-done = bf16[256,8192]{1,0:T(8,128)(2,1)} async-done(((bf16[256,256]{1,0:T(8,128)(2,1)}), bf16[256,8192]{1,0:T(8,128)(2,1)}) %all-gather.3.cloned.1.call-update) | async-done | bytes 4194320 | tf_op jit(solution)/shard_map/all_gather | solution.py:23
  93.9 114.1 %all-gather.5.cloned.1.call-done = bf16[8192,3,256]{0,2,1:T(8,128)(2,1)} async-done(((bf16[512,3,256]{0,2,1:T(8,128)(2,1)}), bf16[8192,3,256]{0,2,1:T(8,128)(2,1)}) %all-gather.5.cloned.1.call-update) | async-done | bytes 12582928 | tf_op jit(solution)/shard_map/all_gather | solution.py:24
  208.0 0.0 copy-start
  208.0 9.3 %convolution_convert_fusion = bf16[256,768]{1,0:T(8,128)(2,1)S(1)} fusion(bf16[256,8192]{1,0:T(8,128)(2,1)} %all-gather.3.cloned.1.call-done, bf16[8192,768]{0,1:T(8,128)(2,1)} %bitcast.45), kind=kOutput, calls=%fused_computation.10 | convolution fusion | flops 3221422080 | bytes 17170432 | tf_op jit(solution)/shard_map/dot_general | solution.py:26
  217.3 0.2 copy.12
  217.5 2.2 collective-permute-start
  219.7 0.0 copy-done
  219.8 0.2 copy.9
  219.9 7.3 %collective-permute-done = bf16[6,3,256]{0,2,1:T(8,128)(2,1)S(1)} collective-permute-done((bf16[6,3,256]{0,2,1:T(8,128)(2,1)S(1)}, bf16[6,3,256]{0,2,1:T(8,128)(2,1)S(1)}, u32[]{:S(2)}, u32[]{:S(2)}) %collective-permute-start) | collective-permute-done | bytes 9248 | tf_op jit(solution)/shard_map/ppermute | solution.py:10
  227.3 2.7 %fusion.3 = f32[256,3,256]{0,2,1:T(8,128)S(1)} fusion(f32[256,3,256]{0,2,1:T(8,128)S(1)} %bitcast.35, f32[6,3,256]{0,2,1:T(8,128)S(1)} %convert_multiply_fusion, f32[3,256]{1,0:T(4,128)S(1)} %get-tuple-element.19, f32[3,256]{1,0:T(4,128)S(1)} %get-tuple-element.20, f32[3,256]{1,0:T(4,128)S(1)} %get-tuple-element.21, f32[3,256]{1,0:T(4,128)S(1)} %get-tuple-element.22, ...), kind=kLoop, calls=%fused_computation.19 | loop fusion | flops 3735552 | bytes 1612800 | tf_op jit(solution)/shard_map/add | solution.py:16
  230.1 0.1 slice_bitcast_fusion.1
  230.2 1.9 collective-permute-start.1
  232.1 7.0 %collective-permute-done.1 = f32[6,256]{0,1:T(8,128)S(1)} collective-permute-done((f32[6,256]{0,1:T(8,128)S(1)}, f32[6,256]{0,1:T(8,128)S(1)}, u32[]{:S(2)}, u32[]{:S(2)}) %collective-permute-start.1) | collective-permute-done | bytes 6176 | tf_op jit(solution)/shard_map/ppermute | solution.py:10
  239.2 0.9 fusion.22
  240.1 0.8 copy.11
  (10 shorter events, 0.1 us)
Async XLA Ops:
  6.5 87.4 %all-gather.3.cloned.1.call-start = ((), (), s32[]{:S(2)}) async-start(), calls=%async_computation | async-start | bytes 4325376 | tf_op jit(solution)/shard_map/all_gather | solution.py:23
  7.3 200.7 %all-gather.5.cloned.1.call-start = ((), (), s32[]{:S(2)}) async-start(), calls=%async_computation.1 | async-start | bytes 13369344 | tf_op jit(solution)/shard_map/all_gather | solution.py:24
  208.0 11.7 %copy-start = (f32[7,256]{1,0:T(8,128)S(1)}, f32[7,256]{1,0:T(8,128)}, u32[]{:S(2)}) copy-start(f32[7,256]{1,0:T(8,128)} %param.7) | copy-start | bytes 21508
  217.5 9.8 %collective-permute-start = (bf16[6,3,256]{0,2,1:T(8,128)(2,1)S(1)}, bf16[6,3,256]{0,2,1:T(8,128)(2,1)S(1)}, u32[]{:S(2)}, u32[]{:S(2)}) collective-permute-start(bf16[6,3,256]{0,2,1:T(8,128)(2,1)S(1)} %bitcast.36), channel_id=1, source_target_pairs={{0,32},{32,64},{64,96},{96,128},{128,160},{160,192},{192,224},{224... | collective-permute-start | bytes 27656 | tf_op jit(solution)/shard_map/ppermute | solution.py:10
  230.2 9.0 %collective-permute-start.1 = (f32[6,256]{0,1:T(8,128)S(1)}, f32[6,256]{0,1:T(8,128)S(1)}, u32[]{:S(2)}, u32[]{:S(2)}) collective-permute-start(f32[6,256]{0,1:T(8,128)S(1)} %slice_bitcast_fusion.1), channel_id=1, source_target_pairs={{0,32},{32,64},{64,96},{96,128},{128,160},{160,192},{192,224},{224... | collective-permute-start | bytes 18440 | tf_op jit(solution)/shard_map/ppermute | solution.py:10
Sparse Core Ops, SparseCore 0:
  9.4 84.4 all-gather.2
  96.9 111.0 all-gather.4
where the time goes:
time: 248 us
  waiting for transfers between devices  212 us (85%)
  between operations  13.5 us (5%)
  matrix products  9.31 us (4%)
  local copies, waits for them, and re-layouts  4.56 us (2%)
  starting transfers between devices  4.17 us (2%)
  other arithmetic  3.72 us (2%)
    all_gather x1, waiting for transfers between devices, per_device(): piece = lax.all_gather(w_in, 'row', axis=0, tiled=True)  114 us
    all_gather x1, waiting for transfers between devices, per_device(): strip = lax.all_gather(tokens, 'col', axis=1, tiled=True)  83.2 us
    ppermute x2, waiting for transfers between devices, passed_along(): return lax.ppermute(block, axis, route)  14.3 us
    dot_general x1, matrix products, per_device(): summed = jnp.dot(strip, flat_piece, preferred_element_type=jnp.float32)  9.31 us
  transfers between devices with their start and end apart: 4, of which 4 were waited for; matrix products, arithmetic and copies ran while one was open for 1% of the time, Pallas kernels for 0%

commit v1 on v0

--- a/solution.py
+++ b/solution.py
@@ -2,6 +2,19 @@
 import jax.numpy as jnp
 from jax import lax
 from jax.sharding import PartitionSpec as P
+
+
+def gather_around(x, axis, dim):
+    ways = lax.axis_size(axis)
+    up = [(d, (d + 1) % ways) for d in range(ways)]
+    down = [(d, (d - 1) % ways) for d in range(ways)]
+    earlier, later = ([x], [x])
+    for _ in range(ways // 2):
+        earlier.append(lax.ppermute(earlier[-1], axis, up))
+    for _ in range((ways - 1) // 2):
+        later.append(lax.ppermute(later[-1], axis, down))
+    line = jnp.concatenate([*earlier[::-1], *later[1:]], axis=dim)
+    return jnp.roll(line, (lax.axis_index(axis) - ways // 2) * x.shape[dim], axis=dim)
 
 
 def passed_along(block, axis, distance):
@@ -21,7 +34,7 @@
     rows = tokens.shape[0]
     cols = w_in.shape[2]
     strip = lax.all_gather(tokens, "col", axis=1, tiled=True)
-    piece = lax.all_gather(w_in, "row", axis=0, tiled=True)
+    piece = gather_around(w_in, "row", 0)
     flat_piece = piece.reshape(piece.shape[0], 3 * cols)
     summed = jnp.dot(strip, flat_piece, preferred_element_type=jnp.float32)
     proj = summed.astype(jnp.bfloat16).reshape(rows, 3, cols)

time: 248 us -> 240 us (0.968)
  the two profiles are of different devices: /device:TPU:8 before, /device:TPU:34 now
where the time goes in v1:
time: 240 us; the launch traced here: 238 us
  waiting for transfers between devices  111 us (46%)
  starting transfers between devices  68.4 us (29%)
  local copies, waits for them, and re-layouts  34.2 us (14%)
  between operations  14.1 us (6%)
  matrix products  9.2 us (4%)
    ppermute x8, waiting for transfers between devices, gather_around(): earlier.append(lax.ppermute(earlier[-1], axis, up))  102 us
    ppermute x7, starting transfers between devices, gather_around(): later.append(lax.ppermute(later[-1], axis, down))  46.3 us
    unnamed x50, local copies, waits for them, and re-layouts  27.3 us
    ppermute x8, starting transfers between devices, gather_around(): earlier.append(lax.ppermute(earlier[-1], axis, up))  18.2 us
    ppermute x2, waiting for transfers between devices, passed_along(): return lax.ppermute(block, axis, route)  9.28 us
    dot_general x1, matrix products, per_device(): summed = jnp.dot(strip, flat_piece, preferred_element_type=jnp.float32)  9.2 us
    dynamic_slice x1, local copies, waits for them, and re-layouts, gather_around(): jnp.roll(line, (lax.axis_index(axis) - ways // 2) * x.shape[dim], axis=dim)  5.33 us
  transfers between devices with their start and end apart: 18, of which 10 were waited for; matrix products, arithmetic and copies ran while one was open for 13% of the time, Pallas kernels for 0%

profile of v1, /device:TPU:34, one launch (start us, length us, event | category | flops | bytes accessed | tf_op | source)
XLA Modules:
  0.0 238.4 jit_solution(3290881955986103635)
XLA Ops:
  7.9 3.4 %collective-permute-start = (bf16[512,3,256]{0,2,1:T(8,128)(2,1)S(1)}, bf16[512,3,256]{0,2,1:T(8,128)(2,1)S(1)}, u32[]{:S(2)}, u32[]{:S(2)}) collective-permute-start(bf16[512,3,256]{0,2,1:T(8,128)(2,1)S(1)} %copy.8), channel_id=1, source_target_pairs={{0,32},{32,64},{64,96},{96,128},{128,160},{160,192},{192,224},{224... | collective-permute-start | bytes 2359304 | tf_op jit(solution)/shard_map/ppermute | solution.py:13
  11.4 17.8 %collective-permute-done = bf16[512,3,256]{0,2,1:T(8,128)(2,1)S(1)} collective-permute-done((bf16[512,3,256]{0,2,1:T(8,128)(2,1)S(1)}, bf16[512,3,256]{0,2,1:T(8,128)(2,1)S(1)}, u32[]{:S(2)}, u32[]{:S(2)}) %collective-permute-start) | collective-permute-done | bytes 786464 | tf_op jit(solution)/shard_map/ppermute | solution.py:13
  29.1 3.4 %collective-permute-start.1 = (bf16[512,3,256]{0,2,1:T(8,128)(2,1)S(1)}, bf16[512,3,256]{0,2,1:T(8,128)(2,1)S(1)}, u32[]{:S(2)}, u32[]{:S(2)}) collective-permute-start(bf16[512,3,256]{0,2,1:T(8,128)(2,1)S(1)} %collective-permute-done), channel_id=1, source_target_pairs={{0,32},{32,64},{64,96},{96,128},{128,160},{160,192},{192,224},{224... | collective-permute-start | bytes 2359304 | tf_op jit(solution)/shard_map/ppermute | solution.py:13
  32.5 4.4 %collective-permute-start.8 = (bf16[512,3,256]{0,2,1:T(8,128)(2,1)S(1)}, bf16[512,3,256]{0,2,1:T(8,128)(2,1)S(1)}, u32[]{:S(2)}, u32[]{:S(2)}) collective-permute-start(bf16[512,3,256]{0,2,1:T(8,128)(2,1)S(1)} %copy.8), channel_id=1, source_target_pairs={{0,480},{32,0},{64,32},{96,64},{128,96},{160,128},{192,160},{224,1... | collective-permute-start | bytes 2359304 | tf_op jit(solution)/shard_map/ppermute | solution.py:15
  37.0 14.9 %collective-permute-done.1 = bf16[512,3,256]{0,2,1:T(8,128)(2,1)S(1)} collective-permute-done((bf16[512,3,256]{0,2,1:T(8,128)(2,1)S(1)}, bf16[512,3,256]{0,2,1:T(8,128)(2,1)S(1)}, u32[]{:S(2)}, u32[]{:S(2)}) %collective-permute-start.1) | collective-permute-done | bytes 786464 | tf_op jit(solution)/shard_map/ppermute | solution.py:13
  53.8 7.0 %collective-permute-start.9 = (bf16[512,3,256]{0,2,1:T(8,128)(2,1)S(1)}, bf16[512,3,256]{0,2,1:T(8,128)(2,1)}, u32[]{:S(2)}, u32[]{:S(2)}) collective-permute-start(bf16[512,3,256]{0,2,1:T(8,128)(2,1)S(1)} %collective-permute-done.8), channel_id=1, source_target_pairs={{0,480},{32,0},{64,32},{96,64},{128,96},{160,128},{192,160},{224,1... | collective-permute-start | bytes 2359304 | tf_op jit(solution)/shard_map/ppermute | solution.py:15
  60.8 14.0 %collective-permute-done.2 = bf16[512,3,256]{0,2,1:T(8,128)(2,1)S(1)} collective-permute-done((bf16[512,3,256]{0,2,1:T(8,128)(2,1)S(1)}, bf16[512,3,256]{0,2,1:T(8,128)(2,1)S(1)}, u32[]{:S(2)}, u32[]{:S(2)}) %collective-permute-start.2) | collective-permute-done | bytes 786464 | tf_op jit(solution)/shard_map/ppermute | solution.py:13
  74.7 1.9 collective-permute-start.3
  76.7 7.0 %collective-permute-start.10 = (bf16[512,3,256]{0,2,1:T(8,128)(2,1)}, bf16[512,3,256]{0,2,1:T(8,128)(2,1)}, u32[]{:S(2)}, u32[]{:S(2)}) collective-permute-start(bf16[512,3,256]{0,2,1:T(8,128)(2,1)} %collective-permute-done.9), channel_id=1, source_target_pairs={{0,480},{32,0},{64,32},{96,64},{128,96},{160,128},{192,160},{224,1... | collective-permute-start | bytes 2359304 | tf_op jit(solution)/shard_map/ppermute | solution.py:15
  83.6 13.1 %collective-permute-done.3 = bf16[512,3,256]{0,2,1:T(8,128)(2,1)} collective-permute-done((bf16[512,3,256]{0,2,1:T(8,128)(2,1)S(1)}, bf16[512,3,256]{0,2,1:T(8,128)(2,1)}, u32[]{:S(2)}, u32[]{:S(2)}) %collective-permute-start.3) | collective-permute-done | bytes 786464 | tf_op jit(solution)/shard_map/ppermute | solution.py:13
  98.7 7.0 %collective-permute-start.11 = (bf16[512,3,256]{0,2,1:T(8,128)(2,1)}, bf16[512,3,256]{0,2,1:T(8,128)(2,1)S(1)}, u32[]{:S(2)}, u32[]{:S(2)}) collective-permute-start(bf16[512,3,256]{0,2,1:T(8,128)(2,1)} %collective-permute-done.10), channel_id=1, source_target_pairs={{0,480},{32,0},{64,32},{96,64},{128,96},{160,128},{192,160},{224,1... | collective-permute-start | bytes 2359304 | tf_op jit(solution)/shard_map/ppermute | solution.py:15
  105.7 12.4 %collective-permute-done.4 = bf16[512,3,256]{0,2,1:T(8,128)(2,1)} collective-permute-done((bf16[512,3,256]{0,2,1:T(8,128)(2,1)}, bf16[512,3,256]{0,2,1:T(8,128)(2,1)}, u32[]{:S(2)}, u32[]{:S(2)}) %collective-permute-start.4) | collective-permute-done | bytes 786464 | tf_op jit(solution)/shard_map/ppermute | solution.py:13
  120.9 7.0 %collective-permute-start.12 = (bf16[512,3,256]{0,2,1:T(8,128)(2,1)S(1)}, bf16[512,3,256]{0,2,1:T(8,128)(2,1)}, u32[]{:S(2)}, u32[]{:S(2)}) collective-permute-start(bf16[512,3,256]{0,2,1:T(8,128)(2,1)S(1)} %collective-permute-done.11), channel_id=1, source_target_pairs={{0,480},{32,0},{64,32},{96,64},{128,96},{160,128},{192,160},{224,1... | collective-permute-start | bytes 2359304 | tf_op jit(solution)/shard_map/ppermute | solution.py:15
  127.9 10.5 %collective-permute-done.5 = bf16[512,3,256]{0,2,1:T(8,128)(2,1)S(1)} collective-permute-done((bf16[512,3,256]{0,2,1:T(8,128)(2,1)}, bf16[512,3,256]{0,2,1:T(8,128)(2,1)S(1)}, u32[]{:S(2)}, u32[]{:S(2)}) %collective-permute-start.5) | collective-permute-done | bytes 786464 | tf_op jit(solution)/shard_map/ppermute | solution.py:13
  140.4 7.0 %collective-permute-start.13 = (bf16[512,3,256]{0,2,1:T(8,128)(2,1)}, bf16[512,3,256]{0,2,1:T(8,128)(2,1)}, u32[]{:S(2)}, u32[]{:S(2)}) collective-permute-start(bf16[512,3,256]{0,2,1:T(8,128)(2,1)} %collective-permute-done.12), channel_id=1, source_target_pairs={{0,480},{32,0},{64,32},{96,64},{128,96},{160,128},{192,160},{224,1... | collective-permute-start | bytes 2359304 | tf_op jit(solution)/shard_map/ppermute | solution.py:15
  147.4 10.4 %collective-permute-done.6 = bf16[512,3,256]{0,2,1:T(8,128)(2,1)} collective-permute-done((bf16[512,3,256]{0,2,1:T(8,128)(2,1)S(1)}, bf16[512,3,256]{0,2,1:T(8,128)(2,1)}, u32[]{:S(2)}, u32[]{:S(2)}) %collective-permute-start.6) | collective-permute-done | bytes 786464 | tf_op jit(solution)/shard_map/ppermute | solution.py:13
  160.8 7.1 %collective-permute-start.14 = (bf16[512,3,256]{0,2,1:T(8,128)(2,1)}, bf16[512,3,256]{0,2,1:T(8,128)(2,1)S(1)}, u32[]{:S(2)}, u32[]{:S(2)}) collective-permute-start(bf16[512,3,256]{0,2,1:T(8,128)(2,1)} %collective-permute-done.13), channel_id=1, source_target_pairs={{0,480},{32,0},{64,32},{96,64},{128,96},{160,128},{192,160},{224,1... | collective-permute-start | bytes 2359304 | tf_op jit(solution)/shard_map/ppermute | solution.py:15
  167.9 8.4 %collective-permute-done.7 = bf16[512,3,256]{0,2,1:T(8,128)(2,1)} collective-permute-done((bf16[512,3,256]{0,2,1:T(8,128)(2,1)}, bf16[512,3,256]{0,2,1:T(8,128)(2,1)}, u32[]{:S(2)}, u32[]{:S(2)}) %collective-permute-start.7) | collective-permute-done | bytes 786464 | tf_op jit(solution)/shard_map/ppermute | solution.py:13
  201.7 5.3 %constant_dynamic-slice_fusion = bf16[8192,3,256]{0,2,1:T(8,128)(2,1)} fusion(bf16[16384,3,256]{0,2,1:T(8,128)(2,1)S(1)} %constant_dynamic-update-slice_fusion, s32[]{:T(128)S(6)} %select_n.18), kind=kLoop, calls=%fused_computation.99 | loop fusion | bytes 25165828 | tf_op jit(solution)/shard_map/jit(_roll_dynamic)/dynamic_slice | solution.py:17
  207.0 9.2 %convolution_convert_fusion = bf16[768,256]{1,0:T(8,128)(2,1)S(1)} fusion(bf16[8192,768]{0,1:T(8,128)(2,1)} %bitcast.38, bf16[256,8192]{1,0:T(8,128)(2,1)} %all-gather.2.cloned.1.call-done), kind=kOutput, calls=%fused_computation.5 | convolution fusion | flops 3221422080 | bytes 17170432 | tf_op jit(solution)/shard_map/dot_general | solution.py:39
  216.5 1.9 collective-permute-start.15
  218.6 5.7 %collective-permute-done.15 = bf16[6,3,256]{2,0,1:T(8,128)(2,1)S(1)} collective-permute-done((bf16[6,3,256]{2,0,1:T(8,128)(2,1)S(1)}, bf16[6,3,256]{2,0,1:T(8,128)(2,1)S(1)}, u32[]{:S(2)}, u32[]{:S(2)}) %collective-permute-start.15) | collective-permute-done | bytes 9248 | tf_op jit(solution)/shard_map/ppermute | solution.py:23
  225.1 1.9 collective-permute-start.16
  227.0 3.6 %collective-permute-done.16 = f32[6,256]{1,0:T(8,128)S(1)} collective-permute-done((f32[6,256]{1,0:T(8,128)S(1)}, f32[6,256]{1,0:T(8,128)S(1)}, u32[]{:S(2)}, u32[]{:S(2)}) %collective-permute-start.16) | collective-permute-done | bytes 6176 | tf_op jit(solution)/shard_map/ppermute | solution.py:23
  (78 shorter events, 40.1 us)
Async XLA Ops:
  6.5 200.5 %all-gather.2.cloned.1.call-start = ((), (), s32[]{:S(2)}) async-start(), calls=%async_computation | async-start | bytes 4325376 | tf_op jit(solution)/shard_map/all_gather | solution.py:36
  7.9 21.2 %collective-permute-start = (bf16[512,3,256]{0,2,1:T(8,128)(2,1)S(1)}, bf16[512,3,256]{0,2,1:T(8,128)(2,1)S(1)}, u32[]{:S(2)}, u32[]{:S(2)}) collective-permute-start(bf16[512,3,256]{0,2,1:T(8,128)(2,1)S(1)} %copy.8), channel_id=1, source_target_pairs={{0,32},{32,64},{64,96},{96,128},{128,160},{160,192},{192,224},{224... | collective-permute-start | bytes 2359304 | tf_op jit(solution)/shard_map/ppermute | solution.py:13
  29.1 22.7 %collective-permute-start.1 = (bf16[512,3,256]{0,2,1:T(8,128)(2,1)S(1)}, bf16[512,3,256]{0,2,1:T(8,128)(2,1)S(1)}, u32[]{:S(2)}, u32[]{:S(2)}) collective-permute-start(bf16[512,3,256]{0,2,1:T(8,128)(2,1)S(1)} %collective-permute-done), channel_id=1, source_target_pairs={{0,32},{32,64},{64,96},{96,128},{128,160},{160,192},{192,224},{224... | collective-permute-start | bytes 2359304 | tf_op jit(solution)/shard_map/ppermute | solution.py:13
  32.5 21.3 %collective-permute-start.8 = (bf16[512,3,256]{0,2,1:T(8,128)(2,1)S(1)}, bf16[512,3,256]{0,2,1:T(8,128)(2,1)S(1)}, u32[]{:S(2)}, u32[]{:S(2)}) collective-permute-start(bf16[512,3,256]{0,2,1:T(8,128)(2,1)S(1)} %copy.8), channel_id=1, source_target_pairs={{0,480},{32,0},{64,32},{96,64},{128,96},{160,128},{192,160},{224,1... | collective-permute-start | bytes 2359304 | tf_op jit(solution)/shard_map/ppermute | solution.py:15
  51.9 22.9 %collective-permute-start.2 = (bf16[512,3,256]{0,2,1:T(8,128)(2,1)S(1)}, bf16[512,3,256]{0,2,1:T(8,128)(2,1)S(1)}, u32[]{:S(2)}, u32[]{:S(2)}) collective-permute-start(bf16[512,3,256]{0,2,1:T(8,128)(2,1)S(1)} %collective-permute-done.1), channel_id=1, source_target_pairs={{0,32},{32,64},{64,96},{96,128},{128,160},{160,192},{192,224},{224... | collective-permute-start | bytes 2359304 | tf_op jit(solution)/shard_map/ppermute | solution.py:13
  53.8 22.9 %collective-permute-start.9 = (bf16[512,3,256]{0,2,1:T(8,128)(2,1)S(1)}, bf16[512,3,256]{0,2,1:T(8,128)(2,1)}, u32[]{:S(2)}, u32[]{:S(2)}) collective-permute-start(bf16[512,3,256]{0,2,1:T(8,128)(2,1)S(1)} %collective-permute-done.8), channel_id=1, source_target_pairs={{0,480},{32,0},{64,32},{96,64},{128,96},{160,128},{192,160},{224,1... | collective-permute-start | bytes 2359304 | tf_op jit(solution)/shard_map/ppermute | solution.py:15
  74.7 1.9 copy-start
  74.7 22.1 %collective-permute-start.3 = (bf16[512,3,256]{0,2,1:T(8,128)(2,1)S(1)}, bf16[512,3,256]{0,2,1:T(8,128)(2,1)}, u32[]{:S(2)}, u32[]{:S(2)}) collective-permute-start(bf16[512,3,256]{0,2,1:T(8,128)(2,1)S(1)} %collective-permute-done.2), channel_id=1, source_target_pairs={{0,32},{32,64},{64,96},{96,128},{128,160},{160,192},{192,224},{224... | collective-permute-start | bytes 2359304 | tf_op jit(solution)/shard_map/ppermute | solution.py:13
  76.7 22.1 %collective-permute-start.10 = (bf16[512,3,256]{0,2,1:T(8,128)(2,1)}, bf16[512,3,256]{0,2,1:T(8,128)(2,1)}, u32[]{:S(2)}, u32[]{:S(2)}) collective-permute-start(bf16[512,3,256]{0,2,1:T(8,128)(2,1)} %collective-permute-done.9), channel_id=1, source_target_pairs={{0,480},{32,0},{64,32},{96,64},{128,96},{160,128},{192,160},{224,1... | collective-permute-start | bytes 2359304 | tf_op jit(solution)/shard_map/ppermute | solution.py:15
  96.8 21.3 %collective-permute-start.4 = (bf16[512,3,256]{0,2,1:T(8,128)(2,1)}, bf16[512,3,256]{0,2,1:T(8,128)(2,1)}, u32[]{:S(2)}, u32[]{:S(2)}) collective-permute-start(bf16[512,3,256]{0,2,1:T(8,128)(2,1)} %collective-permute-done.3), channel_id=1, source_target_pairs={{0,32},{32,64},{64,96},{96,128},{128,160},{160,192},{192,224},{224... | collective-permute-start | bytes 2359304 | tf_op jit(solution)/shard_map/ppermute | solution.py:13
  98.7 21.3 %collective-permute-start.11 = (bf16[512,3,256]{0,2,1:T(8,128)(2,1)}, bf16[512,3,256]{0,2,1:T(8,128)(2,1)S(1)}, u32[]{:S(2)}, u32[]{:S(2)}) collective-permute-start(bf16[512,3,256]{0,2,1:T(8,128)(2,1)} %collective-permute-done.10), channel_id=1, source_target_pairs={{0,480},{32,0},{64,32},{96,64},{128,96},{160,128},{192,160},{224,1... | collective-permute-start | bytes 2359304 | tf_op jit(solution)/shard_map/ppermute | solution.py:15
  118.1 20.3 %collective-permute-start.5 = (bf16[512,3,256]{0,2,1:T(8,128)(2,1)}, bf16[512,3,256]{0,2,1:T(8,128)(2,1)S(1)}, u32[]{:S(2)}, u32[]{:S(2)}) collective-permute-start(bf16[512,3,256]{0,2,1:T(8,128)(2,1)} %collective-permute-done.4), channel_id=1, source_target_pairs={{0,32},{32,64},{64,96},{96,128},{128,160},{160,192},{192,224},{224... | collective-permute-start | bytes 2359304 | tf_op jit(solution)/shard_map/ppermute | solution.py:13
  120.9 19.4 %collective-permute-start.12 = (bf16[512,3,256]{0,2,1:T(8,128)(2,1)S(1)}, bf16[512,3,256]{0,2,1:T(8,128)(2,1)}, u32[]{:S(2)}, u32[]{:S(2)}) collective-permute-start(bf16[512,3,256]{0,2,1:T(8,128)(2,1)S(1)} %collective-permute-done.11), channel_id=1, source_target_pairs={{0,480},{32,0},{64,32},{96,64},{128,96},{160,128},{192,160},{224,1... | collective-permute-start | bytes 2359304 | tf_op jit(solution)/shard_map/ppermute | solution.py:15
  138.4 1.9 copy-start.4
  138.4 19.3 %collective-permute-start.6 = (bf16[512,3,256]{0,2,1:T(8,128)(2,1)S(1)}, bf16[512,3,256]{0,2,1:T(8,128)(2,1)}, u32[]{:S(2)}, u32[]{:S(2)}) collective-permute-start(bf16[512,3,256]{0,2,1:T(8,128)(2,1)S(1)} %collective-permute-done.5), channel_id=1, source_target_pairs={{0,32},{32,64},{64,96},{96,128},{128,160},{160,192},{192,224},{224... | collective-permute-start | bytes 2359304 | tf_op jit(solution)/shard_map/ppermute | solution.py:13
  140.4 20.4 %collective-permute-start.13 = (bf16[512,3,256]{0,2,1:T(8,128)(2,1)}, bf16[512,3,256]{0,2,1:T(8,128)(2,1)}, u32[]{:S(2)}, u32[]{:S(2)}) collective-permute-start(bf16[512,3,256]{0,2,1:T(8,128)(2,1)} %collective-permute-done.12), channel_id=1, source_target_pairs={{0,480},{32,0},{64,32},{96,64},{128,96},{160,128},{192,160},{224,1... | collective-permute-start | bytes 2359304 | tf_op jit(solution)/shard_map/ppermute | solution.py:15
  157.7 18.6 %collective-permute-start.7 = (bf16[512,3,256]{0,2,1:T(8,128)(2,1)}, bf16[512,3,256]{0,2,1:T(8,128)(2,1)}, u32[]{:S(2)}, u32[]{:S(2)}) collective-permute-start(bf16[512,3,256]{0,2,1:T(8,128)(2,1)} %collective-permute-done.6), channel_id=1, source_target_pairs={{0,32},{32,64},{64,96},{96,128},{128,160},{160,192},{192,224},{224... | collective-permute-start | bytes 2359304 | tf_op jit(solution)/shard_map/ppermute | solution.py:13
  160.7 32.5 %copy-start.5 = (bf16[512,3,256]{0,2,1:T(8,128)(2,1)S(1)}, bf16[512,3,256]{0,2,1:T(8,128)(2,1)}, u32[]{:S(2)}) copy-start(bf16[512,3,256]{0,2,1:T(8,128)(2,1)} %copy-done.4) | copy-start | bytes 2359300
  160.7 35.1 %copy-start.1 = (bf16[512,3,256]{0,2,1:T(8,128)(2,1)S(1)}, bf16[512,3,256]{0,2,1:T(8,128)(2,1)}, u32[]{:S(2)}) copy-start(bf16[512,3,256]{0,2,1:T(8,128)(2,1)} %copy-done) | copy-start | bytes 2359300
  160.7 38.2 %copy-start.3 = (bf16[512,3,256]{0,2,1:T(8,128)(2,1)S(1)}, bf16[512,3,256]{0,2,1:T(8,128)(2,1)}, u32[]{:S(2)}) copy-start(bf16[512,3,256]{0,2,1:T(8,128)(2,1)} %copy-done.2) | copy-start | bytes 2359300
  160.8 29.8 %collective-permute-start.14 = (bf16[512,3,256]{0,2,1:T(8,128)(2,1)}, bf16[512,3,256]{0,2,1:T(8,128)(2,1)S(1)}, u32[]{:S(2)}, u32[]{:S(2)}) collective-permute-start(bf16[512,3,256]{0,2,1:T(8,128)(2,1)} %collective-permute-done.13), channel_id=1, source_target_pairs={{0,480},{32,0},{64,32},{96,64},{128,96},{160,128},{192,160},{224,1... | collective-permute-start | bytes 2359304 | tf_op jit(solution)/shard_map/ppermute | solution.py:15
  201.6 16.8 %copy-start.6 = (f32[7,256]{1,0:T(8,128)S(1)}, f32[7,256]{1,0:T(8,128)}, u32[]{:S(2)}) copy-start(f32[7,256]{1,0:T(8,128)} %param.7) | copy-start | bytes 21508
  216.5 7.9 %collective-permute-start.15 = (bf16[6,3,256]{2,0,1:T(8,128)(2,1)S(1)}, bf16[6,3,256]{2,0,1:T(8,128)(2,1)S(1)}, u32[]{:S(2)}, u32[]{:S(2)}) collective-permute-start(bf16[6,3,256]{2,0,1:T(8,128)(2,1)S(1)} %copy.13), channel_id=1, source_target_pairs={{0,32},{32,64},{64,96},{96,128},{128,160},{160,192},{192,224},{224... | collective-permute-start | bytes 27656 | tf_op jit(solution)/shard_map/ppermute | solution.py:23
  225.1 5.5 %collective-permute-start.16 = (f32[6,256]{1,0:T(8,128)S(1)}, f32[6,256]{1,0:T(8,128)S(1)}, u32[]{:S(2)}, u32[]{:S(2)}) collective-permute-start(f32[6,256]{1,0:T(8,128)S(1)} %slice_bitcast_fusion.1), channel_id=1, source_target_pairs={{0,32},{32,64},{64,96},{96,128},{128,160},{160,192},{192,224},{224... | collective-permute-start | bytes 18440 | tf_op jit(solution)/shard_map/ppermute | solution.py:23
  (1 other events, 0.9 us)
Sparse Core Ops, SparseCore 0:
  98.9 87.7 all-gather.1
